TPU v7x, 32 devices: a whole 2x2x4 slice. The times are simulated.
32 devices in a mesh: tile: 4 (over z), chan: 4 (over y, x), tm: 2 (over core).
Axes of the slice: x: 2, y: 2, z: 4, core: 2. Of those that a mesh axis runs over, the one named last changes fastest.
Arguments:
- observed_values: bfloat16 [2, 65536, 128], P('tm', ('tile', 'chan')), may hold values from -6 to 6
- observed_tile: int32 [2, 65536, 1], P('tm', ('tile', 'chan')), may hold values from 0 to 3; in each aligned block of 4096 rows (0 to 4095, 4096 to 8191, ..., all dimensions but the last counted through in order) at most 2048 rows name the same one
- observed_cell: int32 [2, 65536], P('tm', ('tile', 'chan')), may hold values from 0 to 2047
- patch_weight: bfloat16 [4, 256, 256], P(None, None, 'chan'), may hold values from -0.1875 to 0.1875
- depth_weight: bfloat16 [9, 256], P(None, 'chan'), may hold values from -2 to 2
- owners: int32 [4, 4], replicated, may hold values from 0 to 3, as said below
Outputs:
- owned: bfloat16 [4, 2, 4, 64, 256], P('tile', 'tm', None, None, 'chan')
Inputs may be any that keep to these rules, and one draw needn't show every extreme that they name: `observed_tile`: in the rows of one device at most 2048 name the same tile. owners[t, j] - t is the same modulo 4 for every t and differs between any two j, so every row and every column of owners is a permutation.
All inputs are finite; a program needn't handle non-finite values.
Results may differ from a plain program's by a relative error of at most 0.014.
Values may be sent and summed in bfloat16 or wider, within the bound.
A program may use at most 64 MiB of HBM per device.

v0:
```python
import functools
import jax
import jax.numpy as jnp
from jax import lax
from jax.experimental import pallas as pl
from jax.experimental.pallas import tpu as pltpu
from jax.sharding import PartitionSpec as P

V = 128
HS = 32
WS = 64


def padded(x, sides, width):
    for axis, dim in sides:
        devices, length = (lax.axis_size(axis), x.shape[dim])
        up = [(i, (i + 1) % devices) for i in range(devices - 1)]
        down = [(j, i) for i, j in up]
        last = lax.slice_in_dim(x, length - width, length, axis=dim)
        first = lax.slice_in_dim(x, 0, width, axis=dim)
        before = lax.ppermute(last, axis, up)
        after = lax.ppermute(first, axis, down)
        x = jnp.concatenate([before, x, after], axis=dim)
    return x


def pack_rows(values, destination, placed, tile_count, capacity):
    match = (destination[:, None] == lax.iota(jnp.int32, tile_count)[None, :]).astype(jnp.int32)
    earlier = jnp.cumsum(match, axis=0) - match
    position = jnp.sum(earlier * match, axis=1)
    slot_index = destination * capacity + position
    width = values.shape[1]
    sent_values = jnp.zeros((tile_count * capacity, width), jnp.bfloat16).at[slot_index].set(values)
    sent_cells = jnp.full((tile_count * capacity,), -1, jnp.int32).at[slot_index].set(placed)
    return (
        sent_values.reshape(tile_count, capacity, width),
        sent_cells.reshape(tile_count, capacity),
    )


def grid_block(arrived_values, arrived_cells, first_cell):
    cell_ids = first_cell + lax.iota(jnp.int32, 128)
    matches = cell_ids[:, None] == arrived_cells[None, :]
    totals = jnp.dot(
        matches.astype(jnp.bfloat16), arrived_values, preferred_element_type=jnp.float32
    )
    counts = jnp.sum(matches.astype(jnp.float32), axis=1)
    return (totals, counts)


def patch_rows(field, weight, row_start, row_count):
    slab = lax.dynamic_slice_in_dim(field, 2 * row_start, 2 * row_count, 0)
    depth_in = field.shape[2]
    result = jnp.zeros((row_count * (field.shape[1] // 2), weight.shape[2]), jnp.float32)
    for tap_row in range(2):
        for tap_col in range(2):
            window = slab[tap_row::2, tap_col::2, :].reshape(-1, depth_in)
            result = result + jnp.dot(
                window, weight[tap_row * 2 + tap_col], preferred_element_type=jnp.float32
            )
    return result.reshape(row_count, field.shape[1] // 2, weight.shape[2])


def local(observed_values, observed_tile, observed_cell, patch_weight, depth_weight, owners):
    tile_count = lax.axis_size("tile")
    slot_count = lax.axis_size("tm")
    values = observed_values[0]
    capacity = 2 * values.shape[0] // tile_count
    sent_values, sent_cells = pack_rows(
        values, observed_tile[0, :, 0], observed_cell[0], tile_count, capacity
    )
    arrived = (
        lax.all_to_all(sent_values, "tile", split_axis=0, concat_axis=0, tiled=True),
        lax.all_to_all(sent_cells, "tile", split_axis=0, concat_axis=0, tiled=True),
    )
    arrived_values = arrived[0].reshape(-1, V)
    arrived_cells = arrived[1].reshape(-1)
    cell_count = HS * WS
    firsts = jnp.arange(cell_count // 128, dtype=jnp.int32) * 128
    totals, counts = lax.map(
        lambda first_cell: grid_block(arrived_values, arrived_cells, first_cell), firsts
    )
    totals = totals.reshape(cell_count, V)
    counts = counts.reshape(cell_count)
    totals, counts = (
        lax.psum(totals.astype(jnp.bfloat16), "chan").astype(jnp.float32),
        lax.psum(counts.astype(jnp.bfloat16), "chan").astype(jnp.float32),
    )
    means = (totals / jnp.maximum(counts, 1.0)[:, None]).astype(jnp.bfloat16)
    means = means.reshape(HS, WS, V)
    out_rows = HS // (2 * slot_count)
    half_cols = WS // 2
    stacked = lax.all_gather(means, "tm", axis=2, tiled=True)
    encoded = patch_rows(stacked, patch_weight, lax.axis_index("tm") * out_rows, out_rows)
    hidden = jax.nn.gelu(encoded).astype(jnp.bfloat16)
    rimmed = padded(hidden, ((("tile", "tm"), 0),), 2)
    widened = jnp.pad(rimmed, ((0, 0), (2, 2), (0, 0))).astype(jnp.float32)
    depth = jnp.zeros(hidden.shape, jnp.float32)
    for tap_row in range(3):
        for tap_col in range(3):
            shifted = widened[
                2 * tap_row : 2 * tap_row + out_rows, 2 * tap_col : 2 * tap_col + half_cols, :
            ]
            depth = depth + shifted * depth_weight[tap_row * 3 + tap_col].astype(jnp.float32)
    latent = (hidden.astype(jnp.float32) + depth).astype(jnp.bfloat16)
    channels = latent.shape[2]
    pieces = latent.reshape(tile_count, -1, channels)
    own_row = lax.dynamic_index_in_dim(owners, lax.axis_index("tile"), 0, keepdims=False)
    order = lax.iota(jnp.int32, tile_count)
    chosen = jnp.sum(
        order[None, :] * (own_row[None, :] == order[:, None]).astype(jnp.int32), axis=1
    )
    outgoing = pieces[chosen]
    received = lax.all_to_all(outgoing, "tile", split_axis=0, concat_axis=0, tiled=True)
    return received.reshape(1, 1, tile_count, -1, channels)


def fused_kernel(
    values_hbm, column_hbm, tile_hbm, cell_hbm, weight_hbm, depth_hbm, owners_hbm, out_ref,
    values_ref, column_ref, tile_ref, cell_ref, depth_ref, owners_ref,
    masked, onehot, position, partial, first, second_src, second, third_src, third,
    count_src, count_in, weights, mean_src, mean_in, means, hidden_src, hidden_all,
    load_sems,
    weight_send, weight_recv, pass_send, pass_recv, count_send, count_recv,
    first_send, first_recv, second_send, second_recv, third_send, third_recv,
    mean_send, mean_recv, hidden_send, hidden_recv,
):
    f32, bf16 = jnp.float32, jnp.bfloat16
    n_tile, n_chan, n_core = (lax.axis_size(a) for a in ("tile", "chan", "tm"))
    me_t, me_c, me_s = (lax.axis_index(a) for a in ("tile", "chan", "tm"))
    rows, width = values_ref.shape
    block = partial.shape[3]
    quarter = block // 4
    half_cols = WS // 2
    flip_x = me_c + 1 - 2 * (me_c % 2)
    flip_y = (me_c + 2) % 4
    diagonal = 3 - me_c
    near = (flip_x, flip_y)
    far = (flip_y, flip_x)
    other = 1 - me_s
    last = n_tile - 1

    def remote(source, target, send, recv, device):
        return pltpu.make_async_remote_copy(
            src_ref=source, dst_ref=target, send_sem=send, recv_sem=recv,
            device_id=device, device_id_type=pl.DeviceIdType.MESH,
        )

    offsets = [
        (a, b, c) for a in range(n_tile) for b in range(n_chan) for c in range(n_core)
    ][1:]

    def at(a, b, c):
        return ((me_t + a) % n_tile, (me_c + b) % n_chan, (me_s + c) % n_core)

    loads = [
        pltpu.make_async_copy(source, target, load_sems.at[i])
        for i, (source, target) in enumerate((
            (weight_hbm, weights.at[me_c]), (column_hbm, column_ref), (cell_hbm, cell_ref),
            (values_hbm, values_ref), (tile_hbm, tile_ref), (depth_hbm, depth_ref),
            (owners_hbm, owners_ref),
        ))
    ]
    for load in loads:
        load.start()
    barrier = pltpu.get_barrier_semaphore()
    for offset in offsets:
        pl.semaphore_signal(
            barrier, inc=1, device_id=at(*offset), device_id_type=pl.DeviceIdType.MESH
        )

    def weight_copy(o):
        here = weights.at[me_c, me_s]
        return remote(
            here, here, weight_send.at[o - 1], weight_recv.at[o - 1],
            (me_t, (me_c + o) % n_chan, me_s),
        )

    def pass_copy(o):
        here = weights.at[(me_c - o + n_chan) % n_chan, me_s]
        return remote(
            here, here, pass_send.at[o - 1], pass_recv.at[o - 1], (me_t, me_c, other)
        )

    def count_copy(a, b):
        i = a * n_chan + b
        to = ((me_t + a) % n_tile, (me_c + b) % n_chan, me_s)
        return remote(
            count_src.at[to[0] * n_chan + to[1]], count_in.at[i],
            count_send.at[i], count_recv.at[i], to,
        )

    def first_copy(h, k, m, to):
        return remote(
            partial.at[h, k, m], first.at[h, k, m],
            first_send.at[h, k, m], first_recv.at[h, k, m], (me_t, to, me_s),
        )

    def second_copy(h, m):
        return remote(
            second_src.at[h, m], second.at[h, m],
            second_send.at[h, m], second_recv.at[h, m], (me_t, far[h], me_s),
        )

    def third_copy(h, m):
        return remote(
            third_src.at[h, m], third.at[h, m],
            third_send.at[h, m], third_recv.at[h, m],
            ((me_t + m + 1) % n_tile, me_c, me_s),
        )

    loads[1].wait()
    loads[2].wait()
    cell = cell_ref[...]
    row, col = cell // WS, cell % WS
    position[...] = (
        (row // 4) * block + (row % 2) * (2 * quarter) + (col % 2) * quarter
        + ((row % 4) // 2) * half_cols + col // 2
    )
    columns = jnp.transpose(column_ref[...].astype(f32))
    loads[0].wait()
    loads[3].wait()
    for i in range(rows // 128):
        tiles = jnp.broadcast_to(columns[:, i:i + 1], (128, width))
        taken = values_ref[i * 128:(i + 1) * 128, :].astype(f32)
        for m in range(n_tile):
            wanted = ((me_t + m + 1) % n_tile).astype(f32)
            masked[i * 128:(i + 1) * 128, m * width:(m + 1) * width] = jnp.where(
                tiles == wanted, taken, 0.0
            ).astype(bf16)
    ids = lax.broadcasted_iota(jnp.int32, (block, rows), 0)

    def grid_block(k, carry):
        for h in range(2):
            picks = (diagonal, near[h], far[h], me_c)
            j = sum(jnp.where(k == i, p, 0) for i, p in enumerate(picks))
            base = (h * n_chan + j) * block
            onehot[h * block:(h + 1) * block] = (ids == position[...] - base).astype(bf16)
        sums = jnp.dot(onehot[...], masked[...], preferred_element_type=f32)
        for h in range(2):
            for m in range(n_tile):
                partial[h, k, m] = sums[
                    h * block:(h + 1) * block, m * width:(m + 1) * width
                ].astype(bf16)
        return carry

    def do_first(half):
        for k in range(2):
            for m in (2 * half, 2 * half + 1):
                for h in range(2):
                    first_copy(h, k, m, near[h]).start()

    def do_second(half):
        for m in (2 * half, 2 * half + 1):
            for h in range(2):
                first_copy(h, 0, m, near[h]).wait_recv()
                second_src[h, m] = (
                    partial[h, 2, m].astype(f32) + first[h, 0, m].astype(f32)
                ).astype(bf16)
                second_copy(h, m).start()

    def do_third(half):
        for m in (2 * half, 2 * half + 1):
            for h in range(2):
                first_copy(h, 1, m, near[h]).wait_recv()
                second_copy(h, m).wait_recv()
                third_src[h, m] = (
                    partial[h, 3, m].astype(f32)
                    + first[h, 1, m].astype(f32)
                    + second[h, m].astype(f32)
                ).astype(bf16)
                if m != last:
                    third_copy(h, m).start()

    lax.fori_loop(0, 2, grid_block, 0)
    pl.semaphore_wait(barrier, len(offsets))
    do_first(0)
    lax.fori_loop(2, 3, grid_block, 0)
    do_second(0)
    do_first(1)
    lax.fori_loop(3, 4, grid_block, 0)
    do_third(0)
    do_second(1)
    for o in range(1, n_chan):
        weight_copy(o).start()
    loads[4].wait()
    pos = position[...]
    inner = pos % block
    code = (tile_ref[...] * n_chan + (pos // block) % n_chan) * 8
    code = code + (pos // (block * n_chan)) * 2 + inner // 128
    code_ids = lax.broadcasted_iota(jnp.int32, (n_tile * n_chan * 8, rows), 0)
    lane_ids = lax.broadcasted_iota(jnp.int32, (128, rows), 0)
    counts = lax.dot_general(
        (code_ids == code).astype(bf16), (lane_ids == inner % 128).astype(bf16),
        (((1,), (1,)), ((), ())), preferred_element_type=f32,
    )
    count_src[...] = counts.reshape(n_tile * n_chan, 8, 128)
    for a in range(n_tile):
        for b in range(n_chan):
            if a or b:
                count_copy(a, b).start()
    do_third(1)

    here = (me_t * n_core + me_s) * n_chan + me_c
    count = n_tile * n_core * n_chan
    hidden_all[0] = jnp.zeros((half_cols, 128), bf16)
    hidden_all[count + 1] = jnp.zeros((half_cols, 128), bf16)
    loads[5].wait()
    loads[6].wait()
    taps9 = depth_ref[...].astype(f32)
    taps9 = jnp.concatenate([taps9, taps9], axis=1)

    total = count_src[me_t * n_chan + me_c]
    for a in range(n_tile):
        for b in range(n_chan):
            if a or b:
                count_copy(a, b).wait_recv()
                total = total + count_in[a * n_chan + b]
    divisor = jnp.maximum(total, 1.0)

    for o in range(1, n_chan):
        weight_copy(o).wait_recv()
        pass_copy(o).start()
    for h in range(2):
        for m in range(last):
            third_copy(h, m).wait_recv()
        summed = third_src[h, last].astype(f32)
        for m in range(last):
            summed = summed + third[h, m].astype(f32)
        for u in range(block // 128):
            line = divisor[h * 2 + u:h * 2 + u + 1, :]
            each = jnp.transpose(jnp.broadcast_to(line, (128, 128)))
            means[h, u * 128:(u + 1) * 128] = (summed[u * 128:(u + 1) * 128] / each).astype(bf16)

    mean_src[...] = means[other]
    mean_copy = remote(mean_src, mean_in, mean_send, mean_recv, (me_t, me_c, other))
    mean_copy.start()
    for o in range(1, n_chan):
        pass_copy(o).wait_recv()
    mean_copy.wait_recv()
    mine, theirs = means[me_s], mean_in[...]
    even = me_s == 0
    slots = (jnp.where(even, mine, theirs), jnp.where(even, theirs, mine))
    lane = lax.broadcasted_iota(jnp.int32, (half_cols, 128), 1)
    lanes = weights.shape[3]
    for c in range(n_chan):
        taps = []
        for b in range(2):
            acc = jnp.zeros((quarter, 2 * lanes), f32)
            for a in range(2):
                at_row = (2 * a + b) * quarter
                kernel = weights[c, a].reshape(2 * lanes, 2 * width)
                for s in range(2):
                    acc = acc + lax.dot_general(
                        slots[s][at_row:at_row + quarter],
                        kernel[:, s * width:(s + 1) * width],
                        (((1,), (1,)), ((), ())), preferred_element_type=f32,
                    )
            taps.append(acc)
        low = taps[0] + pltpu.roll(taps[1], 64, 1)
        high = pltpu.roll(taps[0], 64, 1) + taps[1]
        encoded = jnp.where(lane < 64, low[:half_cols], high[half_cols:])
        hidden_src[c] = jax.nn.gelu(encoded).astype(bf16)

    def hidden_copy(i):
        to = at(*offsets[i])
        return remote(
            hidden_src.at[to[1]], hidden_all.at[here + 1],
            hidden_send.at[i], hidden_recv.at[i], to,
        )

    def each_hidden(column, act):
        for i, (_, b, c) in enumerate(offsets):
            if c == 0:
                act(hidden_copy(i))
            else:
                @pl.when(column(b) % (n_chan - 1) == 0)
                def _():
                    act(hidden_copy(i))

    each_hidden(lambda b: me_c, lambda copy: copy.start())
    hidden_all[here + 1] = hidden_src[me_c]
    for o in range(1, n_chan):
        weight_copy(o).wait_send()
        pass_copy(o).wait_send()
    for a in range(n_tile):
        for b in range(n_chan):
            if a or b:
                count_copy(a, b).wait_send()
    for m in range(n_tile):
        for h in range(2):
            first_copy(h, 0, m, near[h]).wait_send()
            first_copy(h, 1, m, near[h]).wait_send()
            second_copy(h, m).wait_send()
            if m != last:
                third_copy(h, m).wait_send()
    mean_copy.wait_send()
    each_hidden(lambda b: (me_c + n_chan - b) % n_chan, lambda copy: copy.wait_recv())
    line = lax.broadcasted_iota(jnp.int32, (half_cols, 128), 0)
    for t in range(n_tile):
        j = jnp.int32(0)
        for i in range(n_chan):
            j = jnp.where(owners_ref[t, i] == me_t, i, j)
        at_piece = (t * n_core + me_s) * n_chan + j + 1
        total = jnp.zeros((half_cols, 128), f32)
        for p in range(3):
            field = hidden_all[at_piece + p - 1].astype(f32)
            before = jnp.where(line >= 2, pltpu.roll(field, 2, 0), 0.0)
            after = jnp.where(line < half_cols - 2, pltpu.roll(field, half_cols - 2, 0), 0.0)
            for q, shifted in enumerate((before, field, after)):
                total = total + shifted * taps9[3 * p + q:3 * p + q + 1, :]
            if p == 1:
                middle = field
        latent = middle + total
        out_ref[t, 0:half_cols] = latent[:, :64].astype(bf16)
        out_ref[t, half_cols:] = latent[:, 64:].astype(bf16)
    each_hidden(lambda b: me_c, lambda copy: copy.wait_send())


def fused(observed_values, observed_tile, observed_cell, patch_weight, depth_weight, owners):
    f32, bf16, i32 = jnp.float32, jnp.bfloat16, jnp.int32
    n_tile, n_chan, n_core = (lax.axis_size(a) for a in ("tile", "chan", "tm"))
    values = observed_values[0]
    rows, width = values.shape
    depth_in, lanes = patch_weight.shape[1:]
    turned = jnp.swapaxes(patch_weight, 1, 2).reshape(2, 2, lanes, depth_in)
    block = HS * WS // (n_core * n_chan)
    cells = block // 4
    dma, vmem = pltpu.SemaphoreType.DMA, pltpu.VMEM
    pieces = n_tile * n_core * n_chan
    out = pl.pallas_call(
        fused_kernel,
        out_shape=jax.ShapeDtypeStruct((n_tile, cells, lanes), bf16),
        in_specs=[pl.BlockSpec(memory_space=pl.ANY)] * 7,
        out_specs=pl.BlockSpec(memory_space=pltpu.VMEM),
        scratch_shapes=[
            vmem((rows, width), bf16),
            vmem((rows // 128, 128), i32),
            vmem((1, rows), i32),
            vmem((1, rows), i32),
            vmem(depth_weight.shape, bf16),
            pltpu.SMEM(owners.shape, i32),
            vmem((rows, n_tile * width), bf16),
            vmem((2 * block, rows), bf16),
            vmem((1, rows), i32),
            vmem((2, 4, n_tile, block, width), bf16),
            vmem((2, 2, n_tile, block, width), bf16),
            vmem((2, n_tile, block, width), bf16),
            vmem((2, n_tile, block, width), bf16),
            vmem((2, n_tile, block, width), bf16),
            vmem((2, n_tile, block, width), bf16),
            vmem((n_tile * n_chan, 8, 128), f32),
            vmem((n_tile * n_chan, 8, 128), f32),
            vmem((n_chan, 2, 2, lanes, depth_in), bf16),
            vmem((block, width), bf16),
            vmem((block, width), bf16),
            vmem((2, block, width), bf16),
            vmem((n_chan, cells // 2, 128), bf16),
            vmem((pieces + 2, cells // 2, 128), bf16),
            dma((7,)),
            dma((3,)), dma((3,)), dma((3,)), dma((3,)),
            dma((n_tile * n_chan,)), dma((n_tile * n_chan,)),
            dma((2, 2, n_tile)), dma((2, 2, n_tile)),
            dma((2, n_tile)), dma((2, n_tile)),
            dma((2, n_tile)), dma((2, n_tile)),
            dma, dma,
            dma((pieces - 1,)), dma((pieces - 1,)),
        ],
        compiler_params=pltpu.CompilerParams(
            collective_id=0, has_side_effects=True, vmem_limit_bytes=56 * 2**20
        ),
    )(
        values, observed_tile.reshape(rows // 128, 128), observed_tile.reshape(1, rows),
        observed_cell, turned, depth_weight, owners,
    )
    return out.reshape(1, 1, n_tile, cells, lanes)


def fits(mesh):
    tile, chan, tm = (mesh.shape[a] for a in ("tile", "chan", "tm"))
    return tile == 4 and chan == 4 and tm == 2


def solution(mesh):
    placed = (
        P("tm", ("tile", "chan"), None),
        P("tm", ("tile", "chan"), None),
        P("tm", ("tile", "chan")),
        P(None, None, "chan"),
        P(None, "chan"),
        P(),
    )
    return jax.shard_map(
        fused if fits(mesh) else local,
        mesh=mesh,
        in_specs=placed,
        out_specs=P("tile", "tm", None, None, "chan"),
        check_vma=False,
    )
```

profile of v0, /device:TPU:0, one launch (start us, length us, event | category | flops | bytes accessed | tf_op | source)
XLA Modules:
  0.0 45.7 jit_solution(1989625704746201410)
XLA Ops:
  0.0 44.2 %shard_map.64 = bf16[4,64,64]{2,1,0:T(8,128)(2,1)} custom-call(bf16[4096,128]{1,0:T(8,128)(2,1)} %bitcast.7, s32[32,128]{1,0:T(8,128)} %bitcast.10, s32[1,4096]{1,0:T(1,128)} %bitcast.11, s32[1,4096]{1,0:T(1,128)} %cell_hbm.1, bf16[2,2,64,256]{3,2,1,0:T(8,128)(2,1)} %bitcast.9, bf16[9,64]{1,0:T(8,128)(2,1)} %depth_hbm.1, s32[4,4]{1,0:T(4,128)} %owners_hbm.1), custom_call_target="tpu_custom_call" | custom-call | tf_op jit(solution)/shard_map/pallas_call | solution.py:431
  44.2 1.5 %copy.8 = bf16[1,1,4,64,64]{4,3,2,1,0:T(8,128)(2,1)} copy(bf16[1,1,4,64,64]{4,3,2,1,0:T(8,128)(2,1)} %bitcast.8) | data formatting | bytes 65536
where the time goes:
time: 45.8 us; the launch traced here: 45.7 us
  Pallas kernels  44.2 us (97%)
  local copies, waits for them, and re-layouts  1.47 us (3%)
    pallas_call x1, Pallas kernels, fused(): pl.pallas_call(fused_kernel, out_shape=jax.ShapeDtypeStruct((n_tile, cell...  44.2 us
    unnamed x1, local copies, waits for them, and re-layouts  1.47 us

commit v1 on v0

v1 whole, which is shorter than its diff:
```python
import functools
import jax
import jax.numpy as jnp
from jax import lax
from jax.experimental import pallas as pl
from jax.experimental.pallas import tpu as pltpu
from jax.sharding import PartitionSpec as P

V = 128
HS = 32
WS = 64


def padded(x, sides, width):
    for axis, dim in sides:
        devices, length = (lax.axis_size(axis), x.shape[dim])
        up = [(i, (i + 1) % devices) for i in range(devices - 1)]
        down = [(j, i) for i, j in up]
        last = lax.slice_in_dim(x, length - width, length, axis=dim)
        first = lax.slice_in_dim(x, 0, width, axis=dim)
        before = lax.ppermute(last, axis, up)
        after = lax.ppermute(first, axis, down)
        x = jnp.concatenate([before, x, after], axis=dim)
    return x


def pack_rows(values, destination, placed, tile_count, capacity):
    match = (destination[:, None] == lax.iota(jnp.int32, tile_count)[None, :]).astype(jnp.int32)
    earlier = jnp.cumsum(match, axis=0) - match
    position = jnp.sum(earlier * match, axis=1)
    slot_index = destination * capacity + position
    width = values.shape[1]
    sent_values = jnp.zeros((tile_count * capacity, width), jnp.bfloat16).at[slot_index].set(values)
    sent_cells = jnp.full((tile_count * capacity,), -1, jnp.int32).at[slot_index].set(placed)
    return (
        sent_values.reshape(tile_count, capacity, width),
        sent_cells.reshape(tile_count, capacity),
    )


def grid_block(arrived_values, arrived_cells, first_cell):
    cell_ids = first_cell + lax.iota(jnp.int32, 128)
    matches = cell_ids[:, None] == arrived_cells[None, :]
    totals = jnp.dot(
        matches.astype(jnp.bfloat16), arrived_values, preferred_element_type=jnp.float32
    )
    counts = jnp.sum(matches.astype(jnp.float32), axis=1)
    return (totals, counts)


def patch_rows(field, weight, row_start, row_count):
    slab = lax.dynamic_slice_in_dim(field, 2 * row_start, 2 * row_count, 0)
    depth_in = field.shape[2]
    result = jnp.zeros((row_count * (field.shape[1] // 2), weight.shape[2]), jnp.float32)
    for tap_row in range(2):
        for tap_col in range(2):
            window = slab[tap_row::2, tap_col::2, :].reshape(-1, depth_in)
            result = result + jnp.dot(
                window, weight[tap_row * 2 + tap_col], preferred_element_type=jnp.float32
            )
    return result.reshape(row_count, field.shape[1] // 2, weight.shape[2])


def local(observed_values, observed_tile, observed_cell, patch_weight, depth_weight, owners):
    tile_count = lax.axis_size("tile")
    slot_count = lax.axis_size("tm")
    values = observed_values[0]
    capacity = 2 * values.shape[0] // tile_count
    sent_values, sent_cells = pack_rows(
        values, observed_tile[0, :, 0], observed_cell[0], tile_count, capacity
    )
    arrived = (
        lax.all_to_all(sent_values, "tile", split_axis=0, concat_axis=0, tiled=True),
        lax.all_to_all(sent_cells, "tile", split_axis=0, concat_axis=0, tiled=True),
    )
    arrived_values = arrived[0].reshape(-1, V)
    arrived_cells = arrived[1].reshape(-1)
    cell_count = HS * WS
    firsts = jnp.arange(cell_count // 128, dtype=jnp.int32) * 128
    totals, counts = lax.map(
        lambda first_cell: grid_block(arrived_values, arrived_cells, first_cell), firsts
    )
    totals = totals.reshape(cell_count, V)
    counts = counts.reshape(cell_count)
    totals, counts = (
        lax.psum(totals.astype(jnp.bfloat16), "chan").astype(jnp.float32),
        lax.psum(counts.astype(jnp.bfloat16), "chan").astype(jnp.float32),
    )
    means = (totals / jnp.maximum(counts, 1.0)[:, None]).astype(jnp.bfloat16)
    means = means.reshape(HS, WS, V)
    out_rows = HS // (2 * slot_count)
    half_cols = WS // 2
    stacked = lax.all_gather(means, "tm", axis=2, tiled=True)
    encoded = patch_rows(stacked, patch_weight, lax.axis_index("tm") * out_rows, out_rows)
    hidden = jax.nn.gelu(encoded).astype(jnp.bfloat16)
    rimmed = padded(hidden, ((("tile", "tm"), 0),), 2)
    widened = jnp.pad(rimmed, ((0, 0), (2, 2), (0, 0))).astype(jnp.float32)
    depth = jnp.zeros(hidden.shape, jnp.float32)
    for tap_row in range(3):
        for tap_col in range(3):
            shifted = widened[
                2 * tap_row : 2 * tap_row + out_rows, 2 * tap_col : 2 * tap_col + half_cols, :
            ]
            depth = depth + shifted * depth_weight[tap_row * 3 + tap_col].astype(jnp.float32)
    latent = (hidden.astype(jnp.float32) + depth).astype(jnp.bfloat16)
    channels = latent.shape[2]
    pieces = latent.reshape(tile_count, -1, channels)
    own_row = lax.dynamic_index_in_dim(owners, lax.axis_index("tile"), 0, keepdims=False)
    order = lax.iota(jnp.int32, tile_count)
    chosen = jnp.sum(
        order[None, :] * (own_row[None, :] == order[:, None]).astype(jnp.int32), axis=1
    )
    outgoing = pieces[chosen]
    received = lax.all_to_all(outgoing, "tile", split_axis=0, concat_axis=0, tiled=True)
    return received.reshape(1, 1, tile_count, -1, channels)


def fused_kernel(
    values_hbm, column_hbm, tile_hbm, cell_hbm, weight_hbm, depth_hbm, owners_hbm, out_ref,
    values_ref, column_ref, tile_ref, cell_ref, depth_ref, owners_ref,
    masked, onehot, position, partial, first, second_src, second, third_src, third,
    count_src, count_in, weights, means, hidden_src, hidden_all,
    load_sems, send_sems, recv_sems, first_recv, second_recv, third_recv,
):
    f32, bf16 = jnp.float32, jnp.bfloat16
    n_tile, n_chan, n_core = (lax.axis_size(a) for a in ("tile", "chan", "tm"))
    me_t, me_c, me_s = (lax.axis_index(a) for a in ("tile", "chan", "tm"))
    rows, width = values_ref.shape
    block = partial.shape[3]
    quarter = block // 4
    half_cols = WS // 2
    flip_x = me_c + 1 - 2 * (me_c % 2)
    flip_y = (me_c + 2) % 4
    diagonal = 3 - me_c
    near = (flip_x, flip_y)
    far = (flip_y, flip_x)
    other = 1 - me_s
    shifts = (2, 1, 3, 0)
    own = n_tile - 1
    sends = {n: send_sems.at[i] for i, n in enumerate(SENDS)}
    recvs = {n: recv_sems.at[i] for i, n in enumerate(RECVS)}

    def remote(source, target, send, recv, device):
        return pltpu.make_async_remote_copy(
            src_ref=source, dst_ref=target, send_sem=send, recv_sem=recv,
            device_id=device, device_id_type=pl.DeviceIdType.MESH,
        )

    def all_of(ref, send, recv):
        return remote(ref, ref, send, recv, (me_t, me_c, other))

    offsets = [
        (a, b, c) for a in range(n_tile) for b in range(n_chan) for c in range(n_core)
    ][1:]
    offsets = sorted(offsets, key=lambda o: (2, 1, 3, 0).index(o[0]))

    def at(a, b, c):
        return ((me_t + a) % n_tile, (me_c + b) % n_chan, (me_s + c) % n_core)

    loads = [
        pltpu.make_async_copy(source, target, load_sems.at[i])
        for i, (source, target) in enumerate((
            (weight_hbm, weights.at[:, :, me_c]), (column_hbm, column_ref), (cell_hbm, cell_ref),
            (values_hbm, values_ref), (tile_hbm, tile_ref), (depth_hbm, depth_ref),
            (owners_hbm, owners_ref),
        ))
    ]
    for i in (2, 1, 3, 0, 4, 5, 6):
        loads[i].start()
    barrier = pltpu.get_barrier_semaphore()
    for offset in offsets:
        pl.semaphore_signal(
            barrier, inc=1, device_id=at(*offset), device_id_type=pl.DeviceIdType.MESH
        )

    def weight_copy(o):
        here = weights.at[me_s, :, me_c]
        return remote(
            here, here, sends["weight"], recvs["weight"], (me_t, (me_c + o) % n_chan, me_s)
        )

    def pass_copy(o):
        here = weights.at[me_s, :, (me_c - o + n_chan) % n_chan]
        return remote(here, here, sends["pass"], recvs["pass"], (me_t, me_c, other))

    def count_copy(a, b, c):
        to = at(a, b, c)
        return remote(
            count_src.at[(to[0] * n_chan + to[1]) * n_core + to[2]],
            count_in.at[(c * n_tile + a) * n_chan + b],
            sends["count"], recvs["count"], to,
        )

    def first_copy(h, k, q):
        return remote(
            partial.at[h, k, q], first.at[h, k, q],
            sends["first"], first_recv.at[k, q], (me_t, near[h], me_s),
        )

    def second_copy(h, q):
        return remote(
            second_src.at[h, q], second.at[h, q],
            sends["second"], second_recv.at[q], (me_t, far[h], me_s),
        )

    def third_copy(h, q):
        return remote(
            third_src.at[h, q], third.at[q, me_s], sends["third"], third_recv.at[q],
            ((me_t + shifts[q]) % n_tile, me_c, h),
        )

    loads[2].wait()
    cell = cell_ref[...]
    row, col = cell // WS, cell % WS
    position[...] = (
        (row // 4) * block + (row % 2) * (2 * quarter) + (col % 2) * quarter
        + ((row % 4) // 2) * half_cols + col // 2
    )
    loads[1].wait()
    columns = jnp.transpose(column_ref[...].astype(f32))
    loads[3].wait()

    def mask_rows(pair):
        for i in range(rows // 128):
            tiles = jnp.broadcast_to(columns[:, i:i + 1], (128, width))
            taken = values_ref[i * 128:(i + 1) * 128, :].astype(f32)
            for u in range(2):
                wanted = ((me_t + shifts[2 * pair + u]) % n_tile).astype(f32)
                masked[pair, i * 128:(i + 1) * 128, u * width:(u + 1) * width] = jnp.where(
                    tiles == wanted, taken, 0.0
                ).astype(bf16)

    ids = lax.broadcasted_iota(jnp.int32, (block, rows), 0)

    def grid_block(pair):
        def step(k, carry):
            if pair == 0:
                for h in range(2):
                    picks = (diagonal, near[h], far[h], me_c)
                    j = sum(jnp.where(k == i, p, 0) for i, p in enumerate(picks))
                    base = (h * n_chan + j) * block
                    onehot[k, h * block:(h + 1) * block] = (
                        ids == position[...] - base
                    ).astype(bf16)
            sums = jnp.dot(onehot[k], masked[pair], preferred_element_type=f32)
            for h in range(2):
                for u in range(2):
                    partial[h, k, 2 * pair + u] = sums[
                        h * block:(h + 1) * block, u * width:(u + 1) * width
                    ].astype(bf16)
            return carry
        return step

    def send_first(k, q):
        for h in range(2):
            first_copy(h, k, q).start()

    def send_second(q):
        all_of(first.at[:, 0, q], sends["first"], first_recv.at[0, q]).wait_recv()
        for h in range(2):
            second_src[h, q] = (
                partial[h, 2, q].astype(f32) + first[h, 0, q].astype(f32)
            ).astype(bf16)
            second_copy(h, q).start()

    def send_third(q):
        all_of(first.at[:, 1, q], sends["first"], first_recv.at[1, q]).wait_recv()
        all_of(second.at[:, q], sends["second"], second_recv.at[q]).wait_recv()
        for h in range(2):
            third_src[h, q] = (
                partial[h, 3, q].astype(f32) + first[h, 1, q].astype(f32)
                + second[h, q].astype(f32)
            ).astype(bf16)
            if q != own:
                third_copy(h, q).start()
        if q == own:
            third_copy_own.start()

    third_copy_own = remote(
        third_src.at[other, own], third.at[own, me_s], sends["third"], third_recv.at[own],
        (me_t, me_c, other),
    )

    mask_rows(0)
    lax.fori_loop(0, 2, grid_block(0), 0)
    pl.semaphore_wait(barrier, len(offsets))
    for k in range(2):
        for q in range(2):
            send_first(k, q)
    mask_rows(1)
    lax.fori_loop(2, 4, grid_block(0), 0)
    lax.fori_loop(0, 2, grid_block(1), 0)
    send_second(0)
    send_second(1)
    send_first(0, 2)
    send_first(1, 2)
    lax.fori_loop(2, 4, grid_block(1), 0)
    loads[4].wait()
    pos = position[...]
    inner = pos % block
    code = (tile_ref[...] * n_chan + (pos // block) % n_chan) * 4
    code = code + (pos // (block * n_chan)) * 2 + inner // 128
    code_ids = lax.broadcasted_iota(jnp.int32, (n_tile * n_chan * 4, rows), 0)
    lane_ids = lax.broadcasted_iota(jnp.int32, (128, rows), 0)
    counts = lax.dot_general(
        (code_ids == code).astype(bf16), (lane_ids == inner % 128).astype(bf16),
        (((1,), (1,)), ((), ())), preferred_element_type=f32,
    )
    count_src[...] = counts.reshape(n_tile * n_chan * n_core, 2, 128)
    send_third(0)
    send_third(1)
    send_second(2)
    send_first(0, 3)
    send_first(1, 3)
    loads[0].wait()
    for o in range(1, n_chan):
        weight_copy(o).start()
    send_third(2)
    send_second(3)
    for offset in offsets:
        count_copy(*offset).start()

    here = (me_t * n_core + me_s) * n_chan + me_c
    count = n_tile * n_core * n_chan
    hidden_all[0] = jnp.zeros((half_cols, 128), bf16)
    hidden_all[count + 1] = jnp.zeros((half_cols, 128), bf16)
    loads[5].wait()
    loads[6].wait()
    taps9 = depth_ref[...].astype(f32)
    taps9 = jnp.concatenate([taps9, taps9], axis=1)

    all_of(weights.at[0, :, 0:n_chan - 1], sends["weight"], recvs["weight"]).wait_recv()
    for o in range(1, n_chan):
        pass_copy(o).start()
    send_third(own)

    all_of(count_in.at[0:len(offsets)], sends["count"], recvs["count"]).wait_recv()
    mine = count_src[here_index(me_t, me_c, me_s, n_chan, n_core)]
    theirs = jnp.zeros(mine.shape, f32)
    for i in range(n_tile * n_chan):
        if i:
            mine = mine + count_in[i]
        theirs = theirs + count_in[n_tile * n_chan + i]

    for q in range(own):
        all_of(third.at[q], sends["third"], third_recv.at[q]).wait_recv()
    third_copy_own.wait_recv()
    for slot, counted in ((me_s, mine), (other, theirs)):
        summed = third[0, slot].astype(f32)
        for q in range(1, own):
            summed = summed + third[q, slot].astype(f32)
        if slot is me_s:
            summed = summed + third_src[me_s, own].astype(f32)
        else:
            summed = summed + third[own, slot].astype(f32)
        divisor = jnp.maximum(counted, 1.0)
        for u in range(block // 128):
            each = jnp.transpose(jnp.broadcast_to(divisor[u:u + 1, :], (128, 128)))
            means[slot, u * 128:(u + 1) * 128] = (summed[u * 128:(u + 1) * 128] / each).astype(bf16)

    all_of(weights.at[0, :, 0:n_chan - 1], sends["pass"], recvs["pass"]).wait_recv()
    lanes = weights.shape[3]
    encoded = jnp.zeros((quarter, n_chan * lanes), f32)
    for a in range(2):
        for b in range(2):
            at_row = (2 * a + b) * quarter
            fields = jnp.concatenate(
                [means[s, at_row:at_row + quarter] for s in range(n_core)], axis=1
            )
            encoded = encoded + lax.dot_general(
                fields, weights[a, b].reshape(n_chan * lanes, n_core * width),
                (((1,), (1,)), ((), ())), preferred_element_type=f32,
            )
    hidden = jax.nn.gelu(encoded)
    lane = lax.broadcasted_iota(jnp.int32, (half_cols, 128), 1)
    for g in range(n_chan // 2):
        upper = hidden[:half_cols, g * 128:(g + 1) * 128]
        lower = hidden[half_cols:, g * 128:(g + 1) * 128]
        hidden_src[2 * g] = jnp.where(lane < 64, upper, pltpu.roll(lower, 64, 1)).astype(bf16)
        hidden_src[2 * g + 1] = jnp.where(lane < 64, pltpu.roll(upper, 64, 1), lower).astype(bf16)

    def hidden_copy(i):
        to = at(*offsets[i])
        return remote(
            hidden_src.at[to[1]], hidden_all.at[here + 1], sends["hidden"], recvs["hidden"], to
        )

    on_edge = me_c % (n_chan - 1) == 0
    for i, (_, b, c) in enumerate(offsets):
        if c == 0:
            hidden_copy(i).start()

    @pl.when(on_edge)
    def _():
        for i, (_, b, c) in enumerate(offsets):
            if c:
                hidden_copy(i).start()

    hidden_all[here + 1] = hidden_src[me_c]
    all_of(first, sends["first"], first_recv.at[0, 0]).wait_send()
    all_of(second, sends["second"], second_recv.at[0]).wait_send()
    all_of(third.at[0:own], sends["third"], third_recv.at[0]).wait_send()
    all_of(third.at[own, 0], sends["third"], third_recv.at[own]).wait_send()
    all_of(weights.at[0, :, 0:n_chan - 1], sends["weight"], recvs["weight"]).wait_send()
    all_of(weights.at[0, :, 0:n_chan - 1], sends["pass"], recvs["pass"]).wait_send()
    all_of(count_in.at[0:len(offsets)], sends["count"], recvs["count"]).wait_send()
    every = n_tile * n_chan
    all_of(
        hidden_all.at[0:every - 1 + 2 * n_tile], sends["hidden"], recvs["hidden"]
    ).wait_recv()
    line = lax.broadcasted_iota(jnp.int32, (half_cols, 128), 0)
    for t in range(n_tile):
        j = jnp.int32(0)
        for i in range(n_chan):
            j = jnp.where(owners_ref[t, i] == me_t, i, j)
        at_piece = (t * n_core + me_s) * n_chan + j + 1
        total = jnp.zeros((half_cols, 128), f32)
        for p in range(3):
            field = hidden_all[at_piece + p - 1].astype(f32)
            before = jnp.where(line >= 2, pltpu.roll(field, 2, 0), 0.0)
            after = jnp.where(line < half_cols - 2, pltpu.roll(field, half_cols - 2, 0), 0.0)
            for q, shifted in enumerate((before, field, after)):
                total = total + shifted * taps9[3 * p + q:3 * p + q + 1, :]
            if p == 1:
                middle = field
        latent = middle + total
        out_ref[t, 0:half_cols] = latent[:, :64].astype(bf16)
        out_ref[t, half_cols:] = latent[:, 64:].astype(bf16)
    all_of(hidden_all.at[0:every - 1], sends["hidden"], recvs["hidden"]).wait_send()

    @pl.when(on_edge)
    def _():
        all_of(hidden_all.at[0:every], sends["hidden"], recvs["hidden"]).wait_send()


def here_index(t, c, s, n_chan, n_core):
    return (t * n_chan + c) * n_core + s


SENDS = ("first", "second", "third", "weight", "pass", "count", "hidden")
RECVS = ("weight", "pass", "count", "hidden")


def fused(observed_values, observed_tile, observed_cell, patch_weight, depth_weight, owners):
    f32, bf16, i32 = jnp.float32, jnp.bfloat16, jnp.int32
    n_tile, n_chan, n_core = (lax.axis_size(a) for a in ("tile", "chan", "tm"))
    values = observed_values[0]
    rows, width = values.shape
    depth_in, lanes = patch_weight.shape[1:]
    turned = jnp.swapaxes(patch_weight, 1, 2).reshape(2, 2, lanes, depth_in)
    block = HS * WS // (n_core * n_chan)
    cells = block // 4
    dma, vmem = pltpu.SemaphoreType.DMA, pltpu.VMEM
    pieces = n_tile * n_core * n_chan
    out = pl.pallas_call(
        fused_kernel,
        out_shape=jax.ShapeDtypeStruct((n_tile, cells, lanes), bf16),
        in_specs=[pl.BlockSpec(memory_space=pl.ANY)] * 7,
        out_specs=pl.BlockSpec(memory_space=pltpu.VMEM),
        scratch_shapes=[
            vmem((rows, width), bf16),
            vmem((rows // 128, 128), i32),
            vmem((1, rows), i32),
            vmem((1, rows), i32),
            vmem(depth_weight.shape, bf16),
            pltpu.SMEM(owners.shape, i32),
            vmem((2, rows, 2 * width), bf16),
            vmem((4, 2 * block, rows), bf16),
            vmem((1, rows), i32),
            vmem((2, 4, n_tile, block, width), bf16),
            vmem((2, 2, n_tile, block, width), bf16),
            vmem((2, n_tile, block, width), bf16),
            vmem((2, n_tile, block, width), bf16),
            vmem((2, n_tile, block, width), bf16),
            vmem((n_tile, 2, block, width), bf16),
            vmem((pieces, 2, 128), f32),
            vmem((pieces, 2, 128), f32),
            vmem((2, 2, n_chan, lanes, depth_in), bf16),
            vmem((2, block, width), bf16),
            vmem((n_chan, cells // 2, 128), bf16),
            vmem((pieces + 2, cells // 2, 128), bf16),
            dma((7,)), dma((len(SENDS),)), dma((len(RECVS),)),
            dma((2, n_tile)), dma((n_tile,)), dma((n_tile,)),
        ],
        compiler_params=pltpu.CompilerParams(
            collective_id=0, has_side_effects=True, vmem_limit_bytes=56 * 2**20
        ),
    )(
        values, observed_tile.reshape(rows // 128, 128), observed_tile.reshape(1, rows),
        observed_cell, turned, depth_weight, owners,
    )
    return out.reshape(1, 1, n_tile, cells, lanes)


def fits(mesh):
    tile, chan, tm = (mesh.shape[a] for a in ("tile", "chan", "tm"))
    return tile == 4 and chan == 4 and tm == 2


def solution(mesh):
    placed = (
        P("tm", ("tile", "chan"), None),
        P("tm", ("tile", "chan"), None),
        P("tm", ("tile", "chan")),
        P(None, None, "chan"),
        P(None, "chan"),
        P(),
    )
    return jax.shard_map(
        fused if fits(mesh) else local,
        mesh=mesh,
        in_specs=placed,
        out_specs=P("tile", "tm", None, None, "chan"),
        check_vma=False,
    )
```

time: 45.8 us -> 44.2 us (0.965); the launches traced: 45.7 us -> 43.6 us
  Pallas kernels: 44.2 us -> 42.1 us
    pallas_call x1, Pallas kernels: 44.2 us -> 42.1 us  [fused(): pl.pallas_call(fused_kernel, out_shape=jax.ShapeDtypeStruct((n_tile, cell...]
where the time goes in v1:
time: 44.2 us; the launch traced here: 43.6 us
  Pallas kernels  42.1 us (95%)
  local copies, waits for them, and re-layouts  1.47 us (3%)
    pallas_call x1, Pallas kernels, fused(): pl.pallas_call(fused_kernel, out_shape=jax.ShapeDtypeStruct((n_tile, cell...  42.1 us
    unnamed x1, local copies, waits for them, and re-layouts  1.47 us

profile of v1, /device:TPU:0, one launch (start us, length us, event | category | flops | bytes accessed | tf_op | source)
XLA Modules:
  0.0 43.6 jit_solution(14955645087093638942)
XLA Ops:
  0.0 42.1 %shard_map.64 = bf16[4,64,64]{2,1,0:T(8,128)(2,1)} custom-call(bf16[4096,128]{1,0:T(8,128)(2,1)} %bitcast.7, s32[32,128]{1,0:T(8,128)} %bitcast.10, s32[1,4096]{1,0:T(1,128)} %bitcast.11, s32[1,4096]{1,0:T(1,128)} %cell_hbm.1, bf16[2,2,64,256]{3,2,1,0:T(8,128)(2,1)} %bitcast.9, bf16[9,64]{1,0:T(8,128)(2,1)} %depth_hbm.1, s32[4,4]{1,0:T(4,128)} %owners_hbm.1), custom_call_target="tpu_custom_call" | custom-call | tf_op jit(solution)/shard_map/pallas_call | solution.py:455
  42.1 1.5 %copy.8 = bf16[1,1,4,64,64]{4,3,2,1,0:T(8,128)(2,1)} copy(bf16[1,1,4,64,64]{4,3,2,1,0:T(8,128)(2,1)} %bitcast.8) | data formatting | bytes 65536

commit v2 on v1

--- a/solution.py
+++ b/solution.py
@@ -118,9 +118,9 @@
 def fused_kernel(
     values_hbm, column_hbm, tile_hbm, cell_hbm, weight_hbm, depth_hbm, owners_hbm, out_ref,
     values_ref, column_ref, tile_ref, cell_ref, depth_ref, owners_ref,
-    masked, onehot, position, partial, first, second_src, second, third_src, third,
+    masked_a, masked_b, onehot_a, onehot_b, onehot_c, onehot_d, position, partial, first, second_src, second, third_src, third,
     count_src, count_in, weights, means, hidden_src, hidden_all,
-    load_sems, send_sems, recv_sems, first_recv, second_recv, third_recv,
+    load_sems, send_sems, recv_sems, first_recv, second_recv, third_recv, relays,
 ):
     f32, bf16 = jnp.float32, jnp.bfloat16
     n_tile, n_chan, n_core = (lax.axis_size(a) for a in ("tile", "chan", "tm"))
@@ -135,6 +135,8 @@
     near = (flip_x, flip_y)
     far = (flip_y, flip_x)
     other = 1 - me_s
+    masked = (masked_a, masked_b)
+    onehot = (onehot_a, onehot_b, onehot_c, onehot_d)
     shifts = (2, 1, 3, 0)
     own = n_tile - 1
     sends = {n: send_sems.at[i] for i, n in enumerate(SENDS)}
@@ -145,6 +147,9 @@
             src_ref=source, dst_ref=target, send_sem=send, recv_sem=recv,
             device_id=device, device_id_type=pl.DeviceIdType.MESH,
         )
+
+    def signal(sem, device):
+        pl.semaphore_signal(sem, inc=1, device_id=device, device_id_type=pl.DeviceIdType.MESH)
 
     def all_of(ref, send, recv):
         return remote(ref, ref, send, recv, (me_t, me_c, other))
@@ -167,11 +172,32 @@
     ]
     for i in (2, 1, 3, 0, 4, 5, 6):
         loads[i].start()
+
+    def signal_near(sem):
+        for o in range(1, n_chan):
+            signal(sem, (me_t, (me_c + o) % n_chan, me_s))
+        signal(sem, (me_t, me_c, other))
+
+        @pl.when(me_t > 0)
+        def _():
+            signal(sem, (me_t - 1, me_c, me_s))
+
+        @pl.when(me_t < n_tile - 1)
+        def _():
+            signal(sem, (me_t + 1, me_c, me_s))
+
+    def wait_near(sem):
+        inner_tile = jnp.where((me_t > 0) & (me_t < n_tile - 1), 1, 0)
+        pl.semaphore_wait(sem, n_chan + 1 + inner_tile)
+
+    def relay(i):
+        if i:
+            wait_near(relays.at[i - 1])
+        if i < RELAYS:
+            signal_near(relays.at[i])
+
     barrier = pltpu.get_barrier_semaphore()
-    for offset in offsets:
-        pl.semaphore_signal(
-            barrier, inc=1, device_id=at(*offset), device_id_type=pl.DeviceIdType.MESH
-        )
+    signal_near(barrier)
 
     def weight_copy(o):
         here = weights.at[me_s, :, me_c]
@@ -216,40 +242,46 @@
         (row // 4) * block + (row % 2) * (2 * quarter) + (col % 2) * quarter
         + ((row % 4) // 2) * half_cols + col // 2
     )
+    loads[0].wait()
+    wait_near(barrier)
+    for o in range(1, n_chan):
+        weight_copy(o).start()
+    relay(0)
     loads[1].wait()
     columns = jnp.transpose(column_ref[...].astype(f32))
     loads[3].wait()
 
     def mask_rows(pair):
         for i in range(rows // 128):
-            tiles = jnp.broadcast_to(columns[:, i:i + 1], (128, width))
-            taken = values_ref[i * 128:(i + 1) * 128, :].astype(f32)
+            tiles = jnp.broadcast_to(columns[:, i:i + 1], (128, width)).astype(bf16)
+            taken = values_ref[i * 128:(i + 1) * 128, :]
             for u in range(2):
-                wanted = ((me_t + shifts[2 * pair + u]) % n_tile).astype(f32)
-                masked[pair, i * 128:(i + 1) * 128, u * width:(u + 1) * width] = jnp.where(
-                    tiles == wanted, taken, 0.0
-                ).astype(bf16)
-
-    ids = lax.broadcasted_iota(jnp.int32, (block, rows), 0)
-
-    def grid_block(pair):
-        def step(k, carry):
-            if pair == 0:
-                for h in range(2):
-                    picks = (diagonal, near[h], far[h], me_c)
-                    j = sum(jnp.where(k == i, p, 0) for i, p in enumerate(picks))
-                    base = (h * n_chan + j) * block
-                    onehot[k, h * block:(h + 1) * block] = (
-                        ids == position[...] - base
-                    ).astype(bf16)
-            sums = jnp.dot(onehot[k], masked[pair], preferred_element_type=f32)
-            for h in range(2):
-                for u in range(2):
-                    partial[h, k, 2 * pair + u] = sums[
-                        h * block:(h + 1) * block, u * width:(u + 1) * width
-                    ].astype(bf16)
-            return carry
-        return step
+                wanted = ((me_t + shifts[2 * pair + u]) % n_tile).astype(f32).astype(bf16)
+                masked[pair][i * 128:(i + 1) * 128, u * width:(u + 1) * width] = jnp.where(
+                    tiles == wanted, taken, jnp.zeros_like(taken)
+                )
+
+    ids = lax.broadcasted_iota(jnp.int32, (block, rows), 0).astype(bf16)
+
+    def mark(k):
+        for h in range(2):
+            j = (diagonal, near[h], far[h], me_c)[k]
+            offset = (position[...] - (h * n_chan + j) * block).astype(bf16)
+            onehot[k][h * block:(h + 1) * block] = jnp.where(
+                ids == offset, jnp.ones((), bf16), jnp.zeros((), bf16)
+            )
+
+    def grid_block(k, pair):
+        sums = [
+            jnp.dot(
+                onehot[k][h * block:(h + 1) * block], masked[pair][...],
+                preferred_element_type=f32,
+            )
+            for h in range(2)
+        ]
+        for h in range(2):
+            for u in range(2):
+                partial[h, k, 2 * pair + u] = sums[h][:, u * width:(u + 1) * width].astype(bf16)
 
     def send_first(k, q):
         for h in range(2):
@@ -282,19 +314,23 @@
     )
 
     mask_rows(0)
-    lax.fori_loop(0, 2, grid_block(0), 0)
-    pl.semaphore_wait(barrier, len(offsets))
-    for k in range(2):
-        for q in range(2):
-            send_first(k, q)
+    mark(0)
+    grid_block(0, 0)
+    send_first(0, 0)
+    send_first(0, 1)
+    relay(1)
+    mark(1)
+    grid_block(1, 0)
+    send_first(1, 0)
+    relay(2)
+    mark(2)
+    grid_block(2, 0)
+    mark(3)
     mask_rows(1)
-    lax.fori_loop(2, 4, grid_block(0), 0)
-    lax.fori_loop(0, 2, grid_block(1), 0)
+    grid_block(3, 0)
     send_second(0)
-    send_second(1)
-    send_first(0, 2)
-    send_first(1, 2)
-    lax.fori_loop(2, 4, grid_block(1), 0)
+    send_first(1, 1)
+    relay(3)
     loads[4].wait()
     pos = position[...]
     inner = pos % block
@@ -307,18 +343,26 @@
         (((1,), (1,)), ((), ())), preferred_element_type=f32,
     )
     count_src[...] = counts.reshape(n_tile * n_chan * n_core, 2, 128)
+    relay(4)
+    for offset in offsets:
+        count_copy(*offset).start()
+    grid_block(0, 1)
+    send_second(1)
+    send_first(0, 2)
+    grid_block(1, 1)
+    send_first(1, 2)
     send_third(0)
+    grid_block(2, 1)
+    grid_block(3, 1)
     send_third(1)
     send_second(2)
     send_first(0, 3)
     send_first(1, 3)
-    loads[0].wait()
+    all_of(weights.at[0, :, 0:n_chan - 1], sends["weight"], recvs["weight"]).wait_recv()
     for o in range(1, n_chan):
-        weight_copy(o).start()
+        pass_copy(o).start()
     send_third(2)
     send_second(3)
-    for offset in offsets:
-        count_copy(*offset).start()
 
     here = (me_t * n_core + me_s) * n_chan + me_c
     count = n_tile * n_core * n_chan
@@ -329,9 +373,6 @@
     taps9 = depth_ref[...].astype(f32)
     taps9 = jnp.concatenate([taps9, taps9], axis=1)
 
-    all_of(weights.at[0, :, 0:n_chan - 1], sends["weight"], recvs["weight"]).wait_recv()
-    for o in range(1, n_chan):
-        pass_copy(o).start()
     send_third(own)
 
     all_of(count_in.at[0:len(offsets)], sends["count"], recvs["count"]).wait_recv()
@@ -439,6 +480,7 @@
 
 SENDS = ("first", "second", "third", "weight", "pass", "count", "hidden")
 RECVS = ("weight", "pass", "count", "hidden")
+RELAYS = 4
 
 
 def fused(observed_values, observed_tile, observed_cell, patch_weight, depth_weight, owners):
@@ -454,7 +496,7 @@
     pieces = n_tile * n_core * n_chan
     out = pl.pallas_call(
         fused_kernel,
-        out_shape=jax.ShapeDtypeStruct((n_tile, cells, lanes), bf16),
+        out_shape=vmem((n_tile, cells, lanes), bf16),
         in_specs=[pl.BlockSpec(memory_space=pl.ANY)] * 7,
         out_specs=pl.BlockSpec(memory_space=pltpu.VMEM),
         scratch_shapes=[
@@ -464,8 +506,8 @@
             vmem((1, rows), i32),
             vmem(depth_weight.shape, bf16),
             pltpu.SMEM(owners.shape, i32),
-            vmem((2, rows, 2 * width), bf16),
-            vmem((4, 2 * block, rows), bf16),
+            *[vmem((rows, 2 * width), bf16)] * 2,
+            *[vmem((2 * block, rows), bf16)] * 4,
             vmem((1, rows), i32),
             vmem((2, 4, n_tile, block, width), bf16),
             vmem((2, 2, n_tile, block, width), bf16),
@@ -481,6 +523,7 @@
             vmem((pieces + 2, cells // 2, 128), bf16),
             dma((7,)), dma((len(SENDS),)), dma((len(RECVS),)),
             dma((2, n_tile)), dma((n_tile,)), dma((n_tile,)),
+            pltpu.SemaphoreType.REGULAR((RELAYS,)),
         ],
         compiler_params=pltpu.CompilerParams(
             collective_id=0, has_side_effects=True, vmem_limit_bytes=56 * 2**20

time: 44.2 us -> 38.9 us (0.88)
  Pallas kernels: 42.1 us -> 38 us
  local copies, waits for them, and re-layouts: 1.47 us -> 0.63 us
    pallas_call x1, Pallas kernels: 42.1 us -> 38 us  [fused(): pl.pallas_call(fused_kernel, out_shape=vmem((n_tile, cells, lanes), bf16)...]
    unnamed x1, local copies, waits for them, and re-layouts: 1.47 us -> 0.63 us
where the time goes in v2:
time: 38.9 us; the launch traced here: 38.7 us
  Pallas kernels  38 us (98%)
  local copies, waits for them, and re-layouts  0.63 us (2%)
    pallas_call x1, Pallas kernels, fused(): pl.pallas_call(fused_kernel, out_shape=vmem((n_tile, cells, lanes), bf16)...  38 us

profile of v2, /device:TPU:0, one launch (start us, length us, event | category | flops | bytes accessed | tf_op | source)
XLA Modules:
  0.0 38.7 jit_solution(8561514233914657866)
XLA Ops:
  0.0 38.0 %shard_map.64 = bf16[4,64,64]{2,1,0:T(8,128)(2,1)S(1)} custom-call(bf16[4096,128]{1,0:T(8,128)(2,1)} %bitcast.8, s32[32,128]{1,0:T(8,128)} %bitcast.10, s32[1,4096]{1,0:T(1,128)} %bitcast.11, s32[1,4096]{1,0:T(1,128)} %cell_hbm.1, bf16[2,2,64,256]{3,2,1,0:T(8,128)(2,1)} %bitcast.9, bf16[9,64]{1,0:T(8,128)(2,1)} %depth_hbm.1, s32[4,4]{1,0:T(4,128)} %owners_hbm.1), custom_call_target="tpu_custom_call" | custom-call | tf_op jit(solution)/shard_map/pallas_call | solution.py:497
  38.0 0.6 %copy.8 = bf16[1,1,4,64,64]{4,3,2,1,0:T(8,128)(2,1)} copy(bf16[1,1,4,64,64]{4,3,2,1,0:T(8,128)(2,1)S(1)} %bitcast.7) | data formatting | bytes 65536

commit v3 on v2

--- a/solution.py
+++ b/solution.py
@@ -118,9 +118,10 @@
 def fused_kernel(
     values_hbm, column_hbm, tile_hbm, cell_hbm, weight_hbm, depth_hbm, owners_hbm, out_ref,
     values_ref, column_ref, tile_ref, cell_ref, depth_ref, owners_ref,
-    masked_a, masked_b, onehot_a, onehot_b, onehot_c, onehot_d, position, partial, first, second_src, second, third_src, third,
+    masked_a, masked_b, onehot_a, onehot_b, onehot_c, onehot_d, position, partial, first, second_src, second, third_src, third, early,
     count_src, count_in, weights, means, hidden_src, hidden_all,
-    load_sems, send_sems, recv_sems, first_recv, second_recv, third_recv, relays,
+    load_sems, send_sems, recv_sems, first_recv, second_recv, third_recv,
+    early_recv, relays,
 ):
     f32, bf16 = jnp.float32, jnp.bfloat16
     n_tile, n_chan, n_core = (lax.axis_size(a) for a in ("tile", "chan", "tm"))
@@ -137,7 +138,9 @@
     other = 1 - me_s
     masked = (masked_a, masked_b)
     onehot = (onehot_a, onehot_b, onehot_c, onehot_d)
-    shifts = (2, 1, 3, 0)
+    shifts = (2, 3, 1, 0)
+    half = block // 2
+    split = 1
     own = n_tile - 1
     sends = {n: send_sems.at[i] for i, n in enumerate(SENDS)}
     recvs = {n: recv_sems.at[i] for i, n in enumerate(RECVS)}
@@ -199,14 +202,13 @@
     barrier = pltpu.get_barrier_semaphore()
     signal_near(barrier)
 
-    def weight_copy(o):
+    def weight_copy(to):
         here = weights.at[me_s, :, me_c]
-        return remote(
-            here, here, sends["weight"], recvs["weight"], (me_t, (me_c + o) % n_chan, me_s)
-        )
-
-    def pass_copy(o):
-        here = weights.at[me_s, :, (me_c - o + n_chan) % n_chan]
+        recv = recvs["cross" if to is diagonal else "weight"]
+        return remote(here, here, sends["weight"], recv, (me_t, to, me_s))
+
+    def pass_copy(of):
+        here = weights.at[me_s, :, of]
         return remote(here, here, sends["pass"], recvs["pass"], (me_t, me_c, other))
 
     def count_copy(a, b, c):
@@ -217,23 +219,39 @@
             sends["count"], recvs["count"], to,
         )
 
+    def kept(q):
+        return pl.ds(half, half) if q == split else pl.ds(0, block)
+
     def first_copy(h, k, q):
         return remote(
-            partial.at[h, k, q], first.at[h, k, q],
+            partial.at[h, k, q, kept(q)], first.at[h, k, q, kept(q)],
             sends["first"], first_recv.at[k, q], (me_t, near[h], me_s),
         )
 
     def second_copy(h, q):
         return remote(
-            second_src.at[h, q], second.at[h, q],
+            second_src.at[h, q, kept(q)], second.at[h, q, kept(q)],
             sends["second"], second_recv.at[q], (me_t, far[h], me_s),
         )
 
     def third_copy(h, q):
         return remote(
-            third_src.at[h, q], third.at[q, me_s], sends["third"], third_recv.at[q],
-            ((me_t + shifts[q]) % n_tile, me_c, h),
-        )
+            third_src.at[h, q, kept(q)], third.at[q, me_s, kept(q)],
+            sends["third"], third_recv.at[q], ((me_t + shifts[q]) % n_tile, me_c, h),
+        )
+
+    def early_copy(h, k):
+        return remote(
+            partial.at[h, k, split, pl.ds(0, half)], early.at[h, k],
+            sends["early"], early_recv.at[k], ((me_t + shifts[split]) % n_tile, me_c, me_s),
+        )
+
+    def send_early(k):
+        for h in range(2):
+            early_copy(h, k).start()
+
+    def wait_early(k):
+        all_of(early.at[:, k], sends["early"], early_recv.at[k]).wait_recv()
 
     loads[2].wait()
     cell = cell_ref[...]
@@ -244,8 +262,8 @@
     )
     loads[0].wait()
     wait_near(barrier)
-    for o in range(1, n_chan):
-        weight_copy(o).start()
+    weight_copy(flip_x).start()
+    weight_copy(flip_y).start()
     relay(0)
     loads[1].wait()
     columns = jnp.transpose(column_ref[...].astype(f32))
@@ -284,25 +302,40 @@
                 partial[h, k, 2 * pair + u] = sums[h][:, u * width:(u + 1) * width].astype(bf16)
 
     def send_first(k, q):
+        if q == own:
+            wait_early(k)
         for h in range(2):
+            if q == own:
+                partial[h, k, q, 0:half] = (
+                    partial[h, k, q, 0:half].astype(f32) + early[h, k].astype(f32)
+                ).astype(bf16)
             first_copy(h, k, q).start()
 
+    def combined(h, k, q, arrived):
+        total = partial[h, k, q, kept(q)].astype(f32)
+        for ref in arrived:
+            total = total + ref[kept(q)].astype(f32)
+        if q == own:
+            total = jnp.concatenate(
+                [total[:half] + early[h, k].astype(f32), total[half:]], axis=0
+            )
+        return total.astype(bf16)
+
     def send_second(q):
-        all_of(first.at[:, 0, q], sends["first"], first_recv.at[0, q]).wait_recv()
+        all_of(first.at[:, 0, q, kept(q)], sends["first"], first_recv.at[0, q]).wait_recv()
+        if q == own:
+            wait_early(2)
         for h in range(2):
-            second_src[h, q] = (
-                partial[h, 2, q].astype(f32) + first[h, 0, q].astype(f32)
-            ).astype(bf16)
+            second_src[h, q, kept(q)] = combined(h, 2, q, (first.at[h, 0, q],))
             second_copy(h, q).start()
 
     def send_third(q):
-        all_of(first.at[:, 1, q], sends["first"], first_recv.at[1, q]).wait_recv()
-        all_of(second.at[:, q], sends["second"], second_recv.at[q]).wait_recv()
+        all_of(first.at[:, 1, q, kept(q)], sends["first"], first_recv.at[1, q]).wait_recv()
+        all_of(second.at[:, q, kept(q)], sends["second"], second_recv.at[q]).wait_recv()
+        if q == own:
+            wait_early(3)
         for h in range(2):
-            third_src[h, q] = (
-                partial[h, 3, q].astype(f32) + first[h, 1, q].astype(f32)
-                + second[h, q].astype(f32)
-            ).astype(bf16)
+            third_src[h, q, kept(q)] = combined(h, 3, q, (first.at[h, 1, q], second.at[h, q]))
             if q != own:
                 third_copy(h, q).start()
         if q == own:
@@ -322,15 +355,22 @@
     mark(1)
     grid_block(1, 0)
     send_first(1, 0)
+    send_first(1, 1)
     relay(2)
+    send_early(0)
+    send_early(1)
     mark(2)
     grid_block(2, 0)
+    send_early(2)
+    send_second(0)
     mark(3)
     mask_rows(1)
     grid_block(3, 0)
-    send_second(0)
-    send_first(1, 1)
+    send_early(3)
+    send_second(1)
     relay(3)
+    grid_block(0, 1)
+    send_first(0, 2)
     loads[4].wait()
     pos = position[...]
     inner = pos % block
@@ -346,21 +386,19 @@
     relay(4)
     for offset in offsets:
         count_copy(*offset).start()
-    grid_block(0, 1)
-    send_second(1)
-    send_first(0, 2)
     grid_block(1, 1)
     send_first(1, 2)
     send_third(0)
+    send_third(1)
     grid_block(2, 1)
-    grid_block(3, 1)
-    send_third(1)
     send_second(2)
     send_first(0, 3)
     send_first(1, 3)
-    all_of(weights.at[0, :, 0:n_chan - 1], sends["weight"], recvs["weight"]).wait_recv()
-    for o in range(1, n_chan):
-        pass_copy(o).start()
+    weight_copy(diagonal).start()
+    grid_block(3, 1)
+    all_of(weights.at[0, :, 0:2], sends["weight"], recvs["weight"]).wait_recv()
+    pass_copy(flip_x).start()
+    pass_copy(flip_y).start()
     send_third(2)
     send_second(3)
 
@@ -373,6 +411,8 @@
     taps9 = depth_ref[...].astype(f32)
     taps9 = jnp.concatenate([taps9, taps9], axis=1)
 
+    all_of(weights.at[0, :, 0], sends["weight"], recvs["cross"]).wait_recv()
+    pass_copy(diagonal).start()
     send_third(own)
 
     all_of(count_in.at[0:len(offsets)], sends["count"], recvs["count"]).wait_recv()
@@ -384,12 +424,13 @@
         theirs = theirs + count_in[n_tile * n_chan + i]
 
     for q in range(own):
-        all_of(third.at[q], sends["third"], third_recv.at[q]).wait_recv()
+        all_of(third.at[q, :, kept(q)], sends["third"], third_recv.at[q]).wait_recv()
     third_copy_own.wait_recv()
     for slot, counted in ((me_s, mine), (other, theirs)):
-        summed = third[0, slot].astype(f32)
-        for q in range(1, own):
-            summed = summed + third[q, slot].astype(f32)
+        summed = third[0, slot].astype(f32) + third[2, slot].astype(f32)
+        summed = jnp.concatenate(
+            [summed[:half], summed[half:] + third[split, slot, half:].astype(f32)], axis=0
+        )
         if slot is me_s:
             summed = summed + third_src[me_s, own].astype(f32)
         else:
@@ -438,10 +479,11 @@
                 hidden_copy(i).start()
 
     hidden_all[here + 1] = hidden_src[me_c]
-    all_of(first, sends["first"], first_recv.at[0, 0]).wait_send()
-    all_of(second, sends["second"], second_recv.at[0]).wait_send()
+    most = pl.ds(0, block - half // n_tile)
+    all_of(first.at[:, :, :, most], sends["first"], first_recv.at[0, 0]).wait_send()
+    all_of(second.at[:, :, most], sends["second"], second_recv.at[0]).wait_send()
     all_of(third.at[0:own], sends["third"], third_recv.at[0]).wait_send()
-    all_of(third.at[own, 0], sends["third"], third_recv.at[own]).wait_send()
+    all_of(early, sends["early"], early_recv.at[0]).wait_send()
     all_of(weights.at[0, :, 0:n_chan - 1], sends["weight"], recvs["weight"]).wait_send()
     all_of(weights.at[0, :, 0:n_chan - 1], sends["pass"], recvs["pass"]).wait_send()
     all_of(count_in.at[0:len(offsets)], sends["count"], recvs["count"]).wait_send()
@@ -478,8 +520,8 @@
     return (t * n_chan + c) * n_core + s
 
 
-SENDS = ("first", "second", "third", "weight", "pass", "count", "hidden")
-RECVS = ("weight", "pass", "count", "hidden")
+SENDS = ("first", "second", "third", "weight", "pass", "count", "hidden", "early")
+RECVS = ("weight", "cross", "pass", "count", "hidden")
 RELAYS = 4
 
 
@@ -515,6 +557,7 @@
             vmem((2, n_tile, block, width), bf16),
             vmem((2, n_tile, block, width), bf16),
             vmem((n_tile, 2, block, width), bf16),
+            vmem((2, 4, block // 2, width), bf16),
             vmem((pieces, 2, 128), f32),
             vmem((pieces, 2, 128), f32),
             vmem((2, 2, n_chan, lanes, depth_in), bf16),
@@ -522,7 +565,7 @@
             vmem((n_chan, cells // 2, 128), bf16),
             vmem((pieces + 2, cells // 2, 128), bf16),
             dma((7,)), dma((len(SENDS),)), dma((len(RECVS),)),
-            dma((2, n_tile)), dma((n_tile,)), dma((n_tile,)),
+            dma((2, n_tile)), dma((n_tile,)), dma((n_tile,)), dma((4,)),
             pltpu.SemaphoreType.REGULAR((RELAYS,)),
         ],
         compiler_params=pltpu.CompilerParams(

time: 38.9 us -> 37.3 us (0.959)
  Pallas kernels: 38 us -> 36.5 us
    pallas_call x1, Pallas kernels: 38 us -> 36.5 us  [fused(): pl.pallas_call(fused_kernel, out_shape=vmem((n_tile, cells, lanes), bf16)...]
where the time goes in v3:
time: 37.3 us; the launch traced here: 37.1 us
  Pallas kernels  36.5 us (98%)
  local copies, waits for them, and re-layouts  0.63 us (2%)
    pallas_call x1, Pallas kernels, fused(): pl.pallas_call(fused_kernel, out_shape=vmem((n_tile, cells, lanes), bf16)...  36.5 us

profile of v3, /device:TPU:0, one launch (start us, length us, event | category | flops | bytes accessed | tf_op | source)
XLA Modules:
  0.0 37.1 jit_solution(3779560195630305826)
XLA Ops:
  0.0 36.5 %shard_map.64 = bf16[4,64,64]{2,1,0:T(8,128)(2,1)S(1)} custom-call(bf16[4096,128]{1,0:T(8,128)(2,1)} %bitcast.8, s32[32,128]{1,0:T(8,128)} %bitcast.10, s32[1,4096]{1,0:T(1,128)} %bitcast.11, s32[1,4096]{1,0:T(1,128)} %cell_hbm.1, bf16[2,2,64,256]{3,2,1,0:T(8,128)(2,1)} %bitcast.9, bf16[9,64]{1,0:T(8,128)(2,1)} %depth_hbm.1, s32[4,4]{1,0:T(4,128)} %owners_hbm.1), custom_call_target="tpu_custom_call" | custom-call | tf_op jit(solution)/shard_map/pallas_call | solution.py:539
  36.5 0.6 %copy.8 = bf16[1,1,4,64,64]{4,3,2,1,0:T(8,128)(2,1)} copy(bf16[1,1,4,64,64]{4,3,2,1,0:T(8,128)(2,1)S(1)} %bitcast.7) | data formatting | bytes 65536

commit v4 on v3

--- a/solution.py
+++ b/solution.py
@@ -121,7 +121,7 @@
     masked_a, masked_b, onehot_a, onehot_b, onehot_c, onehot_d, position, partial, first, second_src, second, third_src, third, early,
     count_src, count_in, weights, means, hidden_src, hidden_all,
     load_sems, send_sems, recv_sems, first_recv, second_recv, third_recv,
-    early_recv, relays,
+    early_recv, hidden_recv, relays,
 ):
     f32, bf16 = jnp.float32, jnp.bfloat16
     n_tile, n_chan, n_core = (lax.axis_size(a) for a in ("tile", "chan", "tm"))
@@ -160,7 +160,6 @@
     offsets = [
         (a, b, c) for a in range(n_tile) for b in range(n_chan) for c in range(n_core)
     ][1:]
-    offsets = sorted(offsets, key=lambda o: (2, 1, 3, 0).index(o[0]))
 
     def at(a, b, c):
         return ((me_t + a) % n_tile, (me_c + b) % n_chan, (me_s + c) % n_core)
@@ -371,6 +370,12 @@
     relay(3)
     grid_block(0, 1)
     send_first(0, 2)
+    grid_block(1, 1)
+    send_first(1, 2)
+    weight_copy(diagonal).start()
+    send_third(0)
+    send_third(1)
+    grid_block(2, 1)
     loads[4].wait()
     pos = position[...]
     inner = pos % block
@@ -386,15 +391,9 @@
     relay(4)
     for offset in offsets:
         count_copy(*offset).start()
-    grid_block(1, 1)
-    send_first(1, 2)
-    send_third(0)
-    send_third(1)
-    grid_block(2, 1)
     send_second(2)
     send_first(0, 3)
     send_first(1, 3)
-    weight_copy(diagonal).start()
     grid_block(3, 1)
     all_of(weights.at[0, :, 0:2], sends["weight"], recvs["weight"]).wait_recv()
     pass_copy(flip_x).start()
@@ -461,22 +460,23 @@
         hidden_src[2 * g] = jnp.where(lane < 64, upper, pltpu.roll(lower, 64, 1)).astype(bf16)
         hidden_src[2 * g + 1] = jnp.where(lane < 64, pltpu.roll(upper, 64, 1), lower).astype(bf16)
 
-    def hidden_copy(i):
-        to = at(*offsets[i])
+    edge = 1 - ((me_c + 1) % n_chan) // 2
+
+    def hidden_copy(a, b):
+        to = at(a, b, 0)
         return remote(
-            hidden_src.at[to[1]], hidden_all.at[here + 1], sends["hidden"], recvs["hidden"], to
-        )
-
-    on_edge = me_c % (n_chan - 1) == 0
-    for i, (_, b, c) in enumerate(offsets):
-        if c == 0:
-            hidden_copy(i).start()
-
-    @pl.when(on_edge)
-    def _():
-        for i, (_, b, c) in enumerate(offsets):
-            if c:
-                hidden_copy(i).start()
+            hidden_src.at[to[1]], hidden_all.at[here + 1], sends["hidden"],
+            hidden_recv.at[edge], to,
+        )
+
+    for a in (2, 1, 3, 0):
+        for b in range(n_chan):
+            if a or b:
+                hidden_copy(a, b).start()
+
+    def swap_copy(t, j):
+        here = hidden_all.at[(t * n_core + me_s) * n_chan + j + 1]
+        return remote(here, here, sends["swap"], recvs["swap"], (me_t, me_c, other))
 
     hidden_all[here + 1] = hidden_src[me_c]
     most = pl.ds(0, block - half // n_tile)
@@ -487,10 +487,25 @@
     all_of(weights.at[0, :, 0:n_chan - 1], sends["weight"], recvs["weight"]).wait_send()
     all_of(weights.at[0, :, 0:n_chan - 1], sends["pass"], recvs["pass"]).wait_send()
     all_of(count_in.at[0:len(offsets)], sends["count"], recvs["count"]).wait_send()
-    every = n_tile * n_chan
-    all_of(
-        hidden_all.at[0:every - 1 + 2 * n_tile], sends["hidden"], recvs["hidden"]
-    ).wait_recv()
+    every = n_tile * n_chan // 2
+
+    def wait_hidden(kind):
+        @pl.when(edge == kind)
+        def _():
+            all_of(
+                hidden_all.at[0:every - 1], sends["hidden"], hidden_recv.at[kind]
+            ).wait_recv()
+
+        @pl.when(edge != kind)
+        def _():
+            all_of(hidden_all.at[0:every], sends["hidden"], hidden_recv.at[kind]).wait_recv()
+
+    wait_hidden(1)
+    for t in range(n_tile):
+        for j in (0, n_chan - 1):
+            swap_copy(t, j).start()
+    wait_hidden(0)
+    all_of(hidden_all.at[0:every], sends["swap"], recvs["swap"]).wait_recv()
     line = lax.broadcasted_iota(jnp.int32, (half_cols, 128), 0)
     for t in range(n_tile):
         j = jnp.int32(0)
@@ -509,19 +524,16 @@
         latent = middle + total
         out_ref[t, 0:half_cols] = latent[:, :64].astype(bf16)
         out_ref[t, half_cols:] = latent[:, 64:].astype(bf16)
-    all_of(hidden_all.at[0:every - 1], sends["hidden"], recvs["hidden"]).wait_send()
-
-    @pl.when(on_edge)
-    def _():
-        all_of(hidden_all.at[0:every], sends["hidden"], recvs["hidden"]).wait_send()
+    all_of(hidden_all.at[0:2 * every - 1], sends["hidden"], hidden_recv.at[0]).wait_send()
+    all_of(hidden_all.at[0:every], sends["swap"], recvs["swap"]).wait_send()
 
 
 def here_index(t, c, s, n_chan, n_core):
     return (t * n_chan + c) * n_core + s
 
 
-SENDS = ("first", "second", "third", "weight", "pass", "count", "hidden", "early")
-RECVS = ("weight", "cross", "pass", "count", "hidden")
+SENDS = ("first", "second", "third", "weight", "pass", "count", "hidden", "early", "swap")
+RECVS = ("weight", "cross", "pass", "count", "swap")
 RELAYS = 4
 
 
@@ -565,7 +577,7 @@
             vmem((n_chan, cells // 2, 128), bf16),
             vmem((pieces + 2, cells // 2, 128), bf16),
             dma((7,)), dma((len(SENDS),)), dma((len(RECVS),)),
-            dma((2, n_tile)), dma((n_tile,)), dma((n_tile,)), dma((4,)),
+            dma((2, n_tile)), dma((n_tile,)), dma((n_tile,)), dma((4,)), dma((2,)),
             pltpu.SemaphoreType.REGULAR((RELAYS,)),
         ],
         compiler_params=pltpu.CompilerParams(

time: 37.3 us -> 35.2 us (0.944)
  Pallas kernels: 36.5 us -> 34.3 us
    pallas_call x1, Pallas kernels: 36.5 us -> 34.3 us  [fused(): pl.pallas_call(fused_kernel, out_shape=vmem((n_tile, cells, lanes), bf16)...]
where the time goes in v4:
time: 35.2 us; the launch traced here: 35 us
  Pallas kernels  34.3 us (97%)
  local copies, waits for them, and re-layouts  0.63 us (2%)
    pallas_call x1, Pallas kernels, fused(): pl.pallas_call(fused_kernel, out_shape=vmem((n_tile, cells, lanes), bf16)...  34.3 us

profile of v4, /device:TPU:0, one launch (start us, length us, event | category | flops | bytes accessed | tf_op | source)
XLA Modules:
  0.0 35.0 jit_solution(16566617358897772626)
XLA Ops:
  0.0 34.3 %shard_map.64 = bf16[4,64,64]{2,1,0:T(8,128)(2,1)S(1)} custom-call(bf16[4096,128]{1,0:T(8,128)(2,1)} %bitcast.8, s32[32,128]{1,0:T(8,128)} %bitcast.10, s32[1,4096]{1,0:T(1,128)} %bitcast.11, s32[1,4096]{1,0:T(1,128)} %cell_hbm.1, bf16[2,2,64,256]{3,2,1,0:T(8,128)(2,1)} %bitcast.9, bf16[9,64]{1,0:T(8,128)(2,1)} %depth_hbm.1, s32[4,4]{1,0:T(4,128)} %owners_hbm.1), custom_call_target="tpu_custom_call" | custom-call | tf_op jit(solution)/shard_map/pallas_call | solution.py:551
  34.3 0.6 %copy.8 = bf16[1,1,4,64,64]{4,3,2,1,0:T(8,128)(2,1)} copy(bf16[1,1,4,64,64]{4,3,2,1,0:T(8,128)(2,1)S(1)} %bitcast.7) | data formatting | bytes 65536
